TPU v7x, 32 devices: a whole 2x2x4 slice. The times are simulated.
32 devices in a mesh: ctx: 4 (over x, core), dp: 2 (over y), tp: 4 (over z).
Axes of the slice: x: 2, y: 2, z: 4, core: 2. Of those that a mesh axis runs over, the one named last changes fastest.
Arguments:
- token_ids: int32 [4, 4], replicated, may hold values from 0 to 50279
- decode_prompt: int32 [4], replicated, may hold values from 0 to 3, as said below
- embedding: bfloat16 [50280, 4096], P('dp', ('ctx', 'tp')), may hold values from -6 to 6
- norm_gain: float32 [4096], replicated, may hold values from 0.1 to 1.9
- w_zx: bfloat16 [2, 128, 64, 4096], P(None, ('tp', 'ctx')), may hold values from -0.09375 to 0.09375
- w_bcdt: bfloat16 [4096, 384], P(None, ('ctx', 'tp')), may hold values from -0.09375 to 0.09375
- conv_x_weight: float32 [4, 128, 64], P(None, ('tp', 'ctx')), may hold values from -3 to 3
- conv_x_bias: float32 [128, 64], P(('tp', 'ctx')), may hold values from -3 to 3
- conv_bc_weight: float32 [4, 256], replicated, may hold values from -3 to 3
- conv_bc_bias: float32 [256], replicated, may hold values from -3 to 3
- dt_bias: float32 [128], P(('tp', 'ctx')), may hold values from -4 to -1
- a_log: float32 [128], P(('tp', 'ctx')), may hold values from 0 to 2.7
- d_skip: float32 [128], P(('tp', 'ctx')), may hold values from 0.5 to 1.5
- gate_norm_gain: float32 [128, 64], P(('tp', 'ctx')), may hold values from 0.1 to 1.9
- w_out: bfloat16 [128, 64, 4096], P(('tp', 'ctx')), may hold values from -0.0625 to 0.0625
- state_parts: bfloat16 [4, 4, 128, 64, 128], P('ctx', 'dp', 'tp'), may hold values from -6 to 6
- seg_rate: float32 [4, 4, 128], P('ctx', 'dp', 'tp'), may hold values from 0 to 4
- x_tail: bfloat16 [4, 3, 128, 64], P('dp', None, ('tp', 'ctx')), may hold values from -6 to 6
- bc_tail: bfloat16 [4, 3, 256], P('dp'), may hold values from -6 to 6
Outputs:
- mixer_out: bfloat16 [4, 4, 4096], P(None, 'dp', ('ctx', 'tp'))
- final_state: float32 [4, 128, 64, 128], P('dp', ('tp', 'ctx'))
Inputs may be any that keep to these rules, and one draw needn't show every extreme that they name: decode_prompt is a permutation of the prompts; slot s is decoded by dp group s // 2, and prompt q is held by dp group q // 2; the 2 prompts held by one dp group are decoded by 2 different dp groups.
All inputs are finite; a program needn't handle non-finite values.
Results may differ from a plain program's by a relative error of at most 0.02.
Values may be sent and summed in bfloat16 or wider, within the bound.
A program may use at most 64 MiB of HBM per device.

v0:
```python
import jax
import jax.numpy as jnp
from jax import lax
from jax.sharding import PartitionSpec as P

HEADS = 128
HEAD_DIM = 64


epsilon = 1e-05


def entering(shard, axis, combine, identity):
    count, here = (lax.axis_size(axis), lax.axis_index(axis))
    everything = lax.all_gather(shard, axis)
    start = jnp.broadcast_to(jnp.asarray(identity, shard.dtype), shard.shape)

    def step(k, before):
        at = count - 1 - k
        reached = at > here
        new = combine(before, everything[at])
        return jnp.where(reached, new, before)

    return lax.fori_loop(0, count, step, start)


def rms_scale(values, gain):
    return values * lax.rsqrt(jnp.mean(values * values, axis=-1, keepdims=True) + epsilon) * gain


def select_rows(picker, values):
    return jnp.tensordot(picker, values, axes=1, precision=lax.Precision.HIGHEST)


def add_rates(earlier, later_one):
    return earlier + later_one


def per_device(
    token_ids,
    decode_prompt,
    embedding,
    norm_gain,
    w_zx,
    w_bcdt,
    conv_x_weight,
    conv_x_bias,
    conv_bc_weight,
    conv_bc_bias,
    dt_bias,
    a_log,
    d_skip,
    gate_norm_gain,
    w_out,
    state_parts,
    seg_rate,
    x_tail,
    bc_tail,
):
    group = lax.axis_index("dp")
    local_count = state_parts.shape[1]
    slot_count = decode_prompt.shape[0]
    head_count = w_zx.shape[1]
    state_width = conv_bc_bias.shape[0] // 2
    after_rates = entering(seg_rate, "ctx", add_rates, jnp.zeros_like(seg_rate))
    seg_weight = jnp.exp(-after_rates[0])
    scaled = seg_weight[:, :, None, None] * state_parts[0].astype(jnp.float32)
    channel_sums = lax.psum_scatter(
        scaled.astype(jnp.bfloat16), "ctx", scatter_dimension=2, tiled=True
    ).astype(jnp.float32)
    combined = lax.all_to_all(
        channel_sums.astype(jnp.bfloat16), "ctx", split_axis=1, concat_axis=2, tiled=True
    ).astype(channel_sums.dtype)
    tails_x = x_tail.astype(jnp.float32)
    tails_bc = bc_tail.astype(jnp.float32)
    own_slots = lax.dynamic_slice_in_dim(decode_prompt, group * local_count, local_count)
    prompt_ids = jnp.arange(slot_count, dtype=jnp.int32)
    every_state, every_x, every_bc = (
        lax.all_gather(combined.astype(jnp.bfloat16), "dp", axis=0, tiled=True).astype(
            combined.dtype
        ),
        lax.all_gather(tails_x.astype(jnp.bfloat16), "dp", axis=0, tiled=True).astype(
            tails_x.dtype
        ),
        lax.all_gather(tails_bc.astype(jnp.bfloat16), "dp", axis=0, tiled=True).astype(
            tails_bc.dtype
        ),
    )
    picker = (own_slots[:, None] == prompt_ids[None, :]).astype(jnp.float32)
    ssm_state = select_rows(picker, every_state)
    x_window = select_rows(picker, every_x)
    bc_window = select_rows(picker, every_bc)
    vocab_rows = embedding.shape[0]
    holder = (decode_prompt[:, None] == prompt_ids[None, :]).astype(jnp.int32)
    slot_tokens = jnp.sum(token_ids[:, None, :] * holder[None], axis=2)
    offset_tokens = slot_tokens - group * vocab_rows
    inside = (offset_tokens >= 0) & (offset_tokens < vocab_rows)
    looked = jnp.take(embedding, jnp.clip(offset_tokens, 0, vocab_rows - 1), axis=0)
    partial_rows = jnp.where(inside[..., None], looked.astype(jnp.float32), 0.0)
    own_rows = lax.psum_scatter(
        partial_rows.astype(jnp.bfloat16), "dp", scatter_dimension=1, tiled=True
    )
    embedded = lax.all_gather(own_rows, ("ctx", "tp"), axis=2, tiled=True)
    steps_count = embedded.shape[0]
    flat_rows = embedded.reshape(-1, embedded.shape[2]).astype(jnp.float32)
    normed = rms_scale(flat_rows, norm_gain).astype(jnp.bfloat16)
    projected = jnp.einsum("rd,khed->krhe", normed, w_zx, preferred_element_type=jnp.float32)
    projected = projected.reshape(
        2, steps_count, local_count, projected.shape[2], projected.shape[3]
    )
    columns = lax.all_gather(
        jnp.dot(normed, w_bcdt, preferred_element_type=jnp.float32),
        ("ctx", "tp"),
        axis=1,
        tiled=True,
    )
    columns = columns.reshape(steps_count, local_count, -1)
    head_block = lax.axis_index("tp") * lax.axis_size("ctx") + lax.axis_index("ctx")
    head_start = 2 * state_width + head_block * head_count
    dt_raw = lax.dynamic_slice_in_dim(columns, head_start, head_count, 2)
    decay_rate = -jnp.exp(a_log)
    gated_steps = []
    for moment in range(steps_count):
        x_window = jnp.concatenate([x_window, projected[1, moment][:, None]], axis=1)
        bc_window = jnp.concatenate(
            [bc_window, columns[moment, :, None, : 2 * state_width]], axis=1
        )
        x_conv = jax.nn.silu(jnp.einsum("pkhe,khe->phe", x_window, conv_x_weight) + conv_x_bias)
        bc_conv = jax.nn.silu(jnp.einsum("pkn,kn->pn", bc_window, conv_bc_weight) + conv_bc_bias)
        step_size = jax.nn.softplus(dt_raw[moment] + dt_bias)
        retain = jnp.exp(step_size * decay_rate)
        ssm_state = (
            retain[:, :, None, None] * ssm_state
            + (step_size[:, :, None] * x_conv)[:, :, :, None] * bc_conv[:, None, None, :state_width]
        )
        output = (
            jnp.einsum("phen,pn->phe", ssm_state, bc_conv[:, state_width:])
            + d_skip[None, :, None] * x_conv
        )
        gated_steps.append(output * jax.nn.silu(projected[0, moment]))
        x_window = x_window[:, 1:]
        bc_window = bc_window[:, 1:]
    gated_all = jnp.stack(gated_steps)
    local_squares = jnp.sum(gated_all * gated_all, axis=(2, 3))
    total_squares = lax.psum(local_squares, ("ctx", "tp"))
    inverse = lax.rsqrt(total_squares / (HEADS * HEAD_DIM) + epsilon)
    normed_out = (gated_all * inverse[:, :, None, None] * gate_norm_gain).astype(jnp.bfloat16)
    partial_out = jnp.einsum("tphe,hed->tpd", normed_out, w_out, preferred_element_type=jnp.float32)
    outer_sum = lax.psum_scatter(
        partial_out.astype(jnp.bfloat16), "ctx", scatter_dimension=2, tiled=True
    ).astype(jnp.float32)
    mixed = lax.psum_scatter(outer_sum, "tp", scatter_dimension=2, tiled=True)
    return (mixed.astype(jnp.bfloat16), ssm_state)


def solution(mesh):
    return jax.shard_map(
        per_device,
        mesh=mesh,
        in_specs=(
            P(),
            P(),
            P("dp", ("ctx", "tp")),
            P(),
            P(None, ("tp", "ctx"), None, None),
            P(None, ("ctx", "tp")),
            P(None, ("tp", "ctx"), None),
            P(("tp", "ctx"), None),
            P(),
            P(),
            P(("tp", "ctx")),
            P(("tp", "ctx")),
            P(("tp", "ctx")),
            P(("tp", "ctx"), None),
            P(("tp", "ctx"), None, None),
            P("ctx", "dp", "tp", None, None),
            P("ctx", "dp", "tp"),
            P("dp", None, ("tp", "ctx"), None),
            P("dp", None, None),
        ),
        out_specs=(P(None, "dp", ("ctx", "tp")), P("dp", ("tp", "ctx"), None, None)),
        check_vma=False,
    )
```

profile of v0, /device:TPU:0, one launch (start us, length us, event | category | flops | bytes accessed | tf_op | source)
XLA Modules:
  0.0 232.6 jit_solution(4422377353734788636)
XLA Ops:
  7.3 6.4 %all-gather = f32[4,2,32]{2,1,0:T(2,128)S(1)} all-gather(f32[1,2,32]{2,1,0:T(2,128)} %param.37), channel_id=2, replica_groups=mesh['ctx'=4,'dp'=2,'tp'=4] {'ctx'}, dimensions={0}, use_global_device_ids=true | all-gather | bytes 1280 | tf_op jit(solution)/shard_map/all_gather | solution.py:15
  13.7 0.1 while.16
  13.9 2.5 %fusion.2 = bf16[2,32,64,128]{3,2,0,1:T(8,128)(2,1)} fusion(bf16[1,2,32,64,128]{4,3,2,1,0:T(8,128)(2,1)} %param.36, f32[2,32]{0,1:T(8,128)S(1)} %copy.185), kind=kLoop, calls=%fused_computation.6 | loop fusion | flops 1572864 | bytes 2097408 | tf_op jit(solution)/shard_map/convert_element_type | solution.py:69
  16.4 0.7 fusion.65
  17.1 0.8 multiply_reduce_fusion.2
  18.1 0.1 copy.177
  18.2 0.1 copy.178
  18.3 6.9 %gather_fusion = bf16[16,256]{1,0:T(8,128)(2,1)S(1)} fusion(bf16[25140,256]{1,0:T(8,128)(2,1)} %param.23, s32[1024]{0:T(1024)S(1)} %pad_clamp_fusion), kind=kCustom, calls=%fused_computation | custom fusion | bytes 16448 | tf_op jit(solution)/shard_map/jit(_take)/gather | solution.py:98
  25.3 5.0 %all-reduce = bf16[4,4,256]{2,0,1:T(4,128)(2,1)S(1)} all-reduce(bf16[4,4,256]{2,0,1:T(4,128)(2,1)S(1)} %select_convert_fusion), channel_id=3, replica_groups=mesh['ctx'=4,'dp'=2,'tp'=4] {'dp'}, use_global_device_ids=true, to_apply=%region_1.2.clone | all-reduce | flops 4096 | bytes 16384
  30.3 1.2 dynamic-slice
  32.2 32.8 %all_gather.21 = bf16[4,2,4096]{2,0,1:T(4,128)(2,1)S(1)} all-gather(bf16[4,2,256]{2,0,1:T(4,128)(2,1)S(1)} %constant_dynamic-slice_fusion), channel_id=1, replica_groups=mesh['ctx'=4,'dp'=2,'tp'=4] {'ctx','tp'}, dimensions={2}, use_global_device_ids=true | all-gather | bytes 69632 | tf_op jit(solution)/shard_map/all_gather | solution.py:103
  65.0 0.1 multiply_reduce_fusion
  65.2 0.7 dynamic_slice.17
  66.0 0.7 exponential_negate_fusion
  66.6 4.6 %all_gather.26 = bf16[4,3,8,64]{3,2,1,0:T(8,128)(2,1)S(1)} all-gather(bf16[2,3,8,64]{3,2,1,0:T(8,128)(2,1)} %param.38), channel_id=1, replica_groups=mesh['ctx'=4,'dp'=2,'tp'=4] {'dp'}, dimensions={0}, use_global_device_ids=true | all-gather | bytes 18432 | tf_op jit(solution)/shard_map/all_gather | solution.py:82
  71.5 0.2 convolution_bitcast_fusion.2
  71.8 6.8 %convolution_bitcast_fusion.1 = f32[2,8,8,64]{3,1,2,0:T(8,128)S(1)} fusion(bf16[2,8,64,4096]{3,2,1,0:T(8,128)(2,1)} %param.25, f32[8,4096]{1,0:T(8,128)S(1)} %reshape.335, f32[4096]{0:T(1024)S(1)} %copy-done.2, f32[8]{0:T(128)S(1)} %rsqrt.15), kind=kOutput, calls=%fused_computation.9 | convolution fusion | flops 67207168 | bytes 8568864 | tf_op jit(solution)/shard_map/rd,khed->krhe/dot_general | solution.py:107
  78.6 28.9 %all-gather.1 = f32[16,24,8]{1,2,0:T(8,128)S(1)} all-gather(f32[1,24,8]{1,2,0:T(8,128)S(1)} %convolution_bitcast_fusion.2), channel_id=1, replica_groups=mesh['ctx'=4,'dp'=2,'tp'=4] {'ctx','tp'}, dimensions={0}, use_global_device_ids=true | all-gather | bytes 13056 | tf_op jit(solution)/shard_map/all_gather | solution.py:111
  107.7 0.2 fusion.26
  107.9 0.1 multiply_exponential_fusion.3
  108.5 0.1 fusion.19
  108.7 0.2 copy.192
  108.8 0.2 copy.197
  109.0 0.2 copy.200
  109.2 0.2 copy.203
  109.3 4.4 %all_gather.27 = bf16[4,3,256]{2,1,0:T(4,128)(2,1)S(1)} all-gather(bf16[2,3,256]{2,1,0:T(4,128)(2,1)S(1)} %copy.193), channel_id=1, replica_groups=mesh['ctx'=4,'dp'=2,'tp'=4] {'dp'}, dimensions={0}, use_global_device_ids=true | all-gather | bytes 9216 | tf_op jit(solution)/shard_map/all_gather | solution.py:85
  113.7 0.2 fusion.55
  114.0 3.4 %all-to-all-start = ((bf16[2,32,16,128]{3,2,0,1:T(8,128)(2,1)}), bf16[2,32,16,128]{3,2,0,1:T(8,128)(2,1)S(1)}, u32[]{:S(2)}, u32[]{:S(2)}) async-start(bf16[2,32,16,128]{3,2,0,1:T(8,128)(2,1)} %reduce-scatter.8.cloned.1.call-done), calls=%async_computation.1 | async-start | bytes 524288 | tf_op jit(solution)/shard_map/all_to_all | solution.py:71
  117.5 5.9 %all-to-all-done = bf16[2,32,16,128]{3,2,0,1:T(8,128)(2,1)S(1)} async-done(((bf16[2,32,16,128]{3,2,0,1:T(8,128)(2,1)}), bf16[2,32,16,128]{3,2,0,1:T(8,128)(2,1)S(1)}, u32[]{:S(2)}, u32[]{:S(2)}) %all-to-all-start) | async-done | bytes 262176 | tf_op jit(solution)/shard_map/all_to_all | solution.py:71
  123.4 8.4 %all_gather.25 = bf16[4,8,64,128]{3,2,1,0:T(8,128)(2,1)S(1)} all-gather(bf16[2,8,64,128]{3,2,1,0:T(8,128)(2,1)S(1)} %bitcast.312), channel_id=1, replica_groups=mesh['ctx'=4,'dp'=2,'tp'=4] {'dp'}, dimensions={0}, use_global_device_ids=true | all-gather | bytes 786432 | tf_op jit(solution)/shard_map/all_gather | solution.py:79
  131.9 3.2 %multiply_add_fusion = (f32[2,8,64,128]{3,0,2,1:T(2,128)S(1)}, bf16[2,8,64,128]{3,0,2,1:T(2,128)(2,1)S(1)}, bf16[2,8,64,128]{3,0,2,1:T(2,128)(2,1)S(1)}, bf16[2,8,64,128]{3,0,2,1:T(2,128)(2,1)S(1)}) fusion(f32[2,128]{1,0:T(2,128)S(1)} %get-tuple-element.228, f32[2,8,64]{0,2,1:T(8,128)S(1)} %copy.203, f32[2,8]{0,1:T(8,128)S(1)} %copy.201, ...), kind=kOutput, calls=%fused_computation.17 | convolution fusion | flops 3014664 | bytes 1855752 | tf_op jit(solution)/shard_map/dot_general | solution.py:32
  135.1 0.3 fusion.81
  135.4 0.3 fusion.4
  135.7 0.3 fusion.6
  136.1 0.3 fusion.8
  136.7 31.9 %psum.7 = f32[4,2]{0,1:T(2,128)S(1)} all-reduce(f32[4,2]{0,1:T(2,128)S(1)} %copy.204), channel_id=1, replica_groups=mesh['ctx'=4,'dp'=2,'tp'=4] {'ctx','tp'}, use_global_device_ids=true, to_apply=%region_7.8 | all-reduce | flops 8 | bytes 64 | tf_op jit(solution)/shard_map/psum | solution.py:145
  168.7 2.9 %fusion = bf16[4,2,4096]{2,0,1:T(4,128)(2,1)S(1)} fusion(bf16[8,64,4096]{2,1,0:T(8,128)(2,1)} %param.35, bf16[4,2,8,64]{3,2,1,0:T(8,128)(2,1)S(1)} %multiply_convert_fusion.1), kind=kOutput, calls=%fused_computation.3 | convolution fusion | flops 33587200 | bytes 4268032 | tf_op jit(solution)/shard_map/tphe,hed->tpd/dot_general | solution.py:148
  171.7 2.9 %copy.279 = bf16[4,2,4096]{0,1,2:T(2,128)(2,1)S(1)} copy(bf16[4,2,4096]{2,0,1:T(4,128)(2,1)S(1)} %fusion) | data formatting | bytes 131072
  174.6 1.8 reshape.378
  176.5 22.4 %reduce-scatter.10.cloned.1.call-done = bf16[1024,8]{1,0:T(8,128)(2,1)} async-done(((bf16[4096,8]{1,0:T(8,128)(2,1)}), bf16[1024,8]{1,0:T(8,128)(2,1)}) %reduce-scatter.10.cloned.1.call-update) | async-done | bytes 16400
  198.9 1.2 reshape.379
  200.1 0.4 copy.280
  200.5 0.5 copy.281
  200.9 1.4 reshape.380
  202.4 22.0 %reduce-scatter.12.cloned.1.call-done = f32[256,8]{1,0:T(8,128)} async-done(((f32[1024,8]{1,0:T(8,128)}), f32[256,8]{1,0:T(8,128)}) %reduce-scatter.12.cloned.1.call-update) | async-done | bytes 8208
  224.4 1.0 reshape.381
  225.4 0.1 copy.282
  225.5 0.6 copy.207
  (80 shorter events, 2.2 us)
Async XLA Ops:
  7.2 64.3 %copy-start = (bf16[4096,24]{0,1:T(8,128)(2,1)S(1)}, bf16[4096,24]{0,1:T(8,128)(2,1)}, u32[]{:S(2)}) copy-start(bf16[4096,24]{0,1:T(8,128)(2,1)} %param.26) | copy-start | bytes 589828
  7.2 64.3 %copy-start.2 = (f32[4096]{0:T(1024)S(1)}, f32[4096]{0:T(1024)}, u32[]{:S(2)}) copy-start(f32[4096]{0:T(1024)} %param.24) | copy-start | bytes 49156
  7.2 106.8 %reduce-scatter.8.cloned.1.call-start = ((), (), s32[]{:S(2)}) async-start(), calls=%async_computation.4 | async-start | bytes 1310720 | tf_op jit(solution)/shard_map/reduce_scatter | solution.py:68
  71.8 36.2 %copy-start.10 = (f32[8]{0:T(128)S(1)}, f32[8]{0:T(128)}, u32[]{:S(2)}) copy-start(f32[8]{0:T(128)} %param.31) | copy-start | bytes 100
  71.8 36.3 %copy-start.7 = (bf16[2,3,256]{2,0,1:T(2,128)(2,1)S(1)}, bf16[2,3,256]{2,0,1:T(2,128)(2,1)}, u32[]{:S(2)}) copy-start(bf16[2,3,256]{2,0,1:T(2,128)(2,1)} %param.39) | copy-start | bytes 9220
  71.8 36.7 %copy-start.4 = (f32[4,8,64]{2,1,0:T(8,128)S(1)}, f32[4,8,64]{2,1,0:T(8,128)}, u32[]{:S(2)}) copy-start(f32[4,8,64]{2,1,0:T(8,128)} %param.27) | copy-start | bytes 24580
  71.8 36.8 %copy-start.3 = (f32[8,64]{1,0:T(8,128)S(1)}, f32[8,64]{1,0:T(8,128)}, u32[]{:S(2)}) copy-start(f32[8,64]{1,0:T(8,128)} %param.28) | copy-start | bytes 6148
  71.8 42.1 %copy-start.6 = (f32[4,256]{1,0:T(4,128)S(1)}, f32[4,256]{1,0:T(4,128)}, u32[]{:S(2)}) copy-start(f32[4,256]{1,0:T(4,128)} %param.29) | copy-start | bytes 12292
  71.8 42.2 %copy-start.8 = (f32[256]{0:T(256)S(1)}, f32[256]{0:T(256)}, u32[]{:S(2)}) copy-start(f32[256]{0:T(256)} %param.30) | copy-start | bytes 3076
  114.0 9.4 %all-to-all-start = ((bf16[2,32,16,128]{3,2,0,1:T(8,128)(2,1)}), bf16[2,32,16,128]{3,2,0,1:T(8,128)(2,1)S(1)}, u32[]{:S(2)}, u32[]{:S(2)}) async-start(bf16[2,32,16,128]{3,2,0,1:T(8,128)(2,1)} %reduce-scatter.8.cloned.1.call-done), calls=%async_computation.1 | async-start | bytes 524288 | tf_op jit(solution)/shard_map/all_to_all | solution.py:71
  117.5 81.4 %reduce-scatter.10.cloned.1.call-start = ((), (), s32[]{:S(2)}) async-start(), calls=%async_computation.5 | async-start | bytes 1310720
  131.9 4.5 %copy-start.9 = (f32[8]{0:T(128)S(1)}, f32[8]{0:T(128)}, u32[]{:S(2)}) copy-start(f32[8]{0:T(128)} %param.33) | copy-start | bytes 100
  131.9 36.8 %copy-start.5 = (f32[8,64]{1,0:T(8,128)S(1)}, f32[8,64]{1,0:T(8,128)}, u32[]{:S(2)}) copy-start(f32[8,64]{1,0:T(8,128)} %param.34) | copy-start | bytes 6148
  135.1 39.5 %copy-start.1 = (f32[2,8,64,128]{3,2,1,0:T(8,128)}, f32[2,8,64,128]{3,2,1,0:T(8,128)S(1)}, u32[]{:S(2)}) copy-start(f32[2,8,64,128]{3,2,1,0:T(8,128)S(1)} %copy.208) | copy-start | bytes 1572868
  176.4 48.0 %reduce-scatter.12.cloned.1.call-start = ((), (), s32[]{:S(2)}) async-start(), calls=%async_computation.6 | async-start | bytes 655360
Sparse Core Ops, SparseCore 0:
  16.5 26.5 reduce-scatter.7
  176.5 22.3 reduce-scatter.9
  202.5 21.8 reduce-scatter.11
where the time goes:
time: 233 us
  blocking collectives  122 us (52%)
  waiting for transfers between devices  50.4 us (22%)
  local copies, waits for them, and re-layouts  20.9 us (9%)
  between operations  14.9 us (6%)
  matrix products  14.7 us (6%)
  other arithmetic  5.73 us (2%)
  starting transfers between devices  3.54 us (2%)
    unnamed x5, waiting for transfers between devices  44.5 us
    all_gather x1, blocking collectives, per_device(): embedded = lax.all_gather(own_rows, ('ctx', 'tp'), axis=2, tiled=True)  32.8 us
    psum x1, blocking collectives, per_device(): total_squares = lax.psum(local_squares, ('ctx', 'tp'))  31.9 us
    all_gather x1, blocking collectives, per_device(): lax.all_gather(jnp.dot(normed, w_bcdt, preferred_element_type=jnp.float32...  28.9 us
    unnamed x36, local copies, waits for them, and re-layouts  11.3 us
    all_gather x1, blocking collectives, per_device(): lax.all_gather(combined.astype(jnp.bfloat16), 'dp', axis=0, tiled=True)  8.41 us
    gather x2, local copies, waits for them, and re-layouts, per_device(): jnp.take(embedding, jnp.clip(offset_tokens, 0, vocab_rows - 1), axis=0)  6.9 us
    dot_general x1, matrix products, per_device(): jnp.einsum('rd,khed->krhe', normed, w_zx, preferred_element_type=jnp.floa...  6.79 us
  transfers between devices with their start and end apart: 4, of which 3 were waited for; matrix products, arithmetic and copies ran while one was open for 9% of the time, Pallas kernels for 0%

commit v1 on v0

--- a/solution.py
+++ b/solution.py
@@ -1,6 +1,10 @@
+import functools
+
 import jax
 import jax.numpy as jnp
 from jax import lax
+from jax.experimental import pallas as pl
+from jax.experimental.pallas import tpu as pltpu
 from jax.sharding import PartitionSpec as P
 
 HEADS = 128
@@ -153,9 +157,533 @@
     return (mixed.astype(jnp.bfloat16), ssm_state)
 
 
+HI = lax.Precision.HIGHEST
+F32 = jnp.float32
+BF16 = jnp.bfloat16
+
+
+def f32_dot(a, b):
+    return jnp.dot(a, b, precision=HI, preferred_element_type=F32)
+
+
+def nt_dot(a, b):
+    return lax.dot_general(a, b, (((1,), (1,)), ((), ())), preferred_element_type=F32)
+
+
+def silu(v):
+    return v / (1.0 + jnp.exp(-v))
+
+
+def softplus(v):
+    return jnp.maximum(v, 0.0) + jnp.log1p(jnp.exp(-jnp.abs(v)))
+
+
+ROW_TILE = 16
+
+
+def gather_kernel(steps, slots, groups, tok_ref, dec_ref, emb_ref, out_ref, buf, tail, sems, tail_sem):
+    vocab = emb_ref.shape[0]
+    whole = vocab // ROW_TILE * ROW_TILE
+    base = lax.axis_index("dp") * vocab
+    per_group = slots // groups
+    tail_copy = None
+    if whole < vocab:
+        tail_copy = pltpu.make_async_copy(emb_ref.at[pl.ds(whole, vocab - whole)], tail, tail_sem)
+        tail_copy.start()
+    copies = []
+    where = []
+    for s in range(slots):
+        q = dec_ref[s]
+        for t in range(steps):
+            row = tok_ref[t, q] - base
+            clipped = jnp.clip(row, 0, vocab - 1)
+            start = jnp.minimum(clipped // ROW_TILE * ROW_TILE, whole - ROW_TILE)
+            start = pl.multiple_of(start, ROW_TILE)
+            i = s * steps + t
+            copy = pltpu.make_async_copy(emb_ref.at[pl.ds(start, ROW_TILE)], buf.at[i], sems.at[i])
+            copy.start()
+            copies.append(copy)
+            where.append((row, start))
+    if tail_copy is not None:
+        tail_copy.wait()
+    for copy in copies:
+        copy.wait()
+    rows = lax.broadcasted_iota(jnp.int32, (ROW_TILE, 1), 0)
+    for g in range(groups):
+        picked = []
+        for t in range(steps):
+            for j in range(per_group):
+                i = (g * per_group + j) * steps + t
+                row, start = where[i]
+                value = jnp.sum(
+                    jnp.where(rows == row - start, buf[i].astype(F32), 0.0), axis=0, keepdims=True
+                )
+                if tail_copy is not None:
+                    trows = lax.broadcasted_iota(jnp.int32, (vocab - whole, 1), 0)
+                    value += jnp.sum(
+                        jnp.where(trows == row - whole, tail[...].astype(F32), 0.0),
+                        axis=0,
+                        keepdims=True,
+                    )
+                picked.append(value)
+        out_ref[g] = jnp.concatenate(picked, axis=0).astype(BF16)
+
+
+def mixer_kernel(
+    sizes,
+    dec_ref,
+    part_ref,
+    gain_ref,
+    cxw_ref,
+    cxb_ref,
+    cbw_ref,
+    cbb_ref,
+    dtb_ref,
+    alog_ref,
+    skip_ref,
+    gg_ref,
+    seg_ref,
+    xt_ref,
+    bt_ref,
+    wzx_hbm,
+    wbc_hbm,
+    wout_hbm,
+    state_hbm,
+    mixed_ref,
+    final_ref,
+    wzx,
+    wbc,
+    wout,
+    state_in,
+    state_send,
+    state_recv,
+    emb_recv,
+    seg_recv,
+    xt_recv,
+    bt_recv,
+    col_send,
+    col_recv,
+    sq_send,
+    sq_recv,
+    out_send,
+    out_recv,
+    start_state,
+    xfull,
+    bcfull,
+    gated_ref,
+    load_sems,
+    own_sem,
+    emb_sems,
+    state_sems,
+    seg_sems,
+    xt_sems,
+    bt_sems,
+    col_sems,
+    sq_sems,
+    out_sems,
+):
+    n_ctx, n_dp, n_tp, total_heads = sizes
+    c, d, p = lax.axis_index("ctx"), lax.axis_index("dp"), lax.axis_index("tp")
+    mine = c * n_tp + p
+    steps, per, feats = mixed_ref.shape
+    rows = steps * per
+    heads, dim = cxb_ref.shape
+    chans = heads * dim
+    width = cbb_ref.shape[1]
+    state_n = width // 2
+    taps = cxw_ref.shape[0]
+    model = gain_ref.shape[1]
+    tp_heads = seg_ref.shape[-1]
+    n_cols = wbc_hbm.shape[1]
+    all_cols = n_cols * n_ctx * n_tp
+
+    loads = []
+    half = wzx_hbm.shape[0] // 2
+    pairs = (
+        (state_hbm, state_in),
+        (wbc_hbm, wbc),
+        (wzx_hbm.at[pl.ds(half, half)], wzx.at[pl.ds(half, half)]),
+        (wzx_hbm.at[pl.ds(0, half)], wzx.at[pl.ds(0, half)]),
+        (wout_hbm, wout),
+    )
+    for i, (source, target) in enumerate(pairs):
+        load = pltpu.make_async_copy(source, target, load_sems.at[i])
+        load.start()
+        loads.append(load)
+
+    def peer(offset):
+        dc, dd, dt = offset
+        return lax.rem(c + dc, n_ctx), lax.rem(d + dd, n_dp), lax.rem(p + dt, n_tp)
+
+    def device(offset):
+        a, b, e = peer(offset)
+        return {"ctx": a, "dp": b, "tp": e}
+
+    everyone = [
+        (a, b, e) for a in range(n_ctx) for b in range(n_dp) for e in range(n_tp) if a + b + e
+    ]
+    everyone.sort(key=lambda o: -(min(o[2], n_tp - o[2]) * 4 + o[1] * 2 + o[0]))
+    group = [o for o in everyone if o[1] == 0]
+    routed = [o for o in everyone if o[2] == 0]
+    across = [o for o in everyone if o[0] == 0 and o[2] == 0]
+
+    barrier = pltpu.get_barrier_semaphore()
+    for o in everyone:
+        pl.semaphore_signal(
+            barrier, inc=1, device_id=device(o), device_id_type=pl.DeviceIdType.MESH
+        )
+
+    def send(source, target, sems, slot, offset):
+        copy = pltpu.make_async_remote_copy(
+            src_ref=source,
+            dst_ref=target,
+            send_sem=sems.at[0, slot],
+            recv_sem=sems.at[1, slot],
+            device_id=device(offset),
+            device_id_type=pl.DeviceIdType.MESH,
+        )
+        copy.start()
+        return copy
+
+    loads[0].wait()
+    for g in range(n_dp):
+        pick = jnp.int32(0)
+        for j in range(per):
+            local = dec_ref[g * per + j] - d * per
+            pick += jnp.where((local >= 0) & (local < per), local, 0)
+        state_send[g] = state_in[pick]
+
+    col_send[...] = jnp.zeros_like(col_send)
+
+    pl.semaphore_wait(barrier, len(everyone))
+
+    emb_copies = [
+        send(part_ref.at[peer(o)[1]], emb_recv.at[d, mine], emb_sems, i, o)
+        for i, o in enumerate(everyone)
+    ]
+    emb_recv[d, mine] = part_ref[d]
+    seg_copies = [send(seg_ref.at[0], seg_recv.at[d, c], seg_sems, i, o) for i, o in enumerate(routed)]
+    xt_copies = [send(xt_ref, xt_recv.at[d], xt_sems, i, o) for i, o in enumerate(across)]
+    bt_copies = [send(bt_ref, bt_recv.at[d], bt_sems, i, o) for i, o in enumerate(across)]
+    state_copies = []
+    for i, o in enumerate(routed):
+        pc, pd, _ = peer(o)
+        source = state_send.at[pd, pl.ds(pl.multiple_of(pc * chans, chans), chans)]
+        state_copies.append(send(source, state_recv.at[d, c], state_sems, i, o))
+    own = pltpu.make_async_copy(
+        state_send.at[d, pl.ds(pl.multiple_of(c * chans, chans), chans)],
+        state_recv.at[d, c],
+        own_sem,
+    )
+    own.start()
+    seg_recv[d, c] = seg_ref[0]
+    xt_recv[d] = xt_ref[...]
+    bt_recv[d] = bt_ref[...]
+
+    lane = lax.broadcasted_iota(jnp.int32, (1, chans), 1)
+    fold = (
+        lax.broadcasted_iota(jnp.int32, (dim, chans), 0)
+        == lax.rem(lax.broadcasted_iota(jnp.int32, (dim, chans), 1), dim)
+    ).astype(F32)
+    head_rows = lax.broadcasted_iota(jnp.int32, (heads, chans), 0) == lax.div(
+        lax.broadcasted_iota(jnp.int32, (heads, chans), 1), dim
+    )
+
+    def flat(value):
+        return jnp.sum(jnp.where(head_rows, f32_dot(value, fold), 0.0), axis=0, keepdims=True)
+
+    def spread(value, first):
+        count = value.shape[1]
+        chosen = (
+            lax.broadcasted_iota(jnp.int32, (count, chans), 0)
+            == first + lax.div(lax.broadcasted_iota(jnp.int32, (count, chans), 1), dim)
+        ).astype(F32)
+        return f32_dot(value, chosen)
+
+    tap_rows = [flat(cxw_ref[k]) for k in range(taps)]
+    bias_row = flat(cxb_ref[...])
+    gate_row = flat(gg_ref[...])
+    dtb_row = spread(dtb_ref[...], 0)
+    rate_row = -jnp.exp(spread(alog_ref[...], 0))
+    skip_row = spread(skip_ref[...], 0)
+
+    for copy in emb_copies:
+        copy.wait_recv()
+    pieces = []
+    for i in range(n_ctx * n_tp):
+        piece = emb_recv[0, i].astype(F32)
+        for g in range(1, n_dp):
+            piece += emb_recv[g, i].astype(F32)
+        pieces.append(piece)
+    embedded = jnp.concatenate(pieces, axis=1)
+    scale = lax.rsqrt(jnp.sum(embedded * embedded, axis=1, keepdims=True) / model + epsilon)
+    normed = (embedded * scale * gain_ref[...]).astype(BF16)
+    loads[1].wait()
+    col_send[:, 0:n_cols] = jnp.dot(normed, wbc[...], preferred_element_type=F32)
+    col_copies = [send(col_send, col_recv.at[mine], col_sems, i, o) for i, o in enumerate(group)]
+    col_recv[mine] = col_send[...]
+    loads[2].wait()
+    x_rows = nt_dot(normed, wzx[half : 2 * half, :])
+    loads[3].wait()
+    z_gate = silu(nt_dot(normed, wzx[0:half, :]))
+
+    for copy in xt_copies + bt_copies:
+        copy.wait_recv()
+    holders = [lax.div(dec_ref[d * per + j], per) for j in range(per)]
+    places = [lax.rem(dec_ref[d * per + j], per) for j in range(per)]
+    for k in range(taps - 1):
+        for j in range(per):
+            r = k * per + j
+            xfull[r : r + 1, :] = flat(xt_recv[holders[j], places[j], k].astype(F32))
+            bcfull[r : r + 1, :] = bt_recv[holders[j], places[j], pl.ds(k, 1), :].astype(F32)
+    lead = (taps - 1) * per
+    xfull[lead : lead + rows, :] = x_rows
+    conv = bias_row
+    for k in range(taps):
+        conv = conv + tap_rows[k] * xfull[k * per : k * per + rows, :]
+    xc = silu(conv)
+
+    for copy in seg_copies:
+        copy.wait_recv()
+    weights = []
+    for j in range(per):
+        after = jnp.zeros((1, tp_heads), F32)
+        ordered = []
+        for k in reversed(range(n_ctx)):
+            ordered.append(jnp.exp(-after))
+            after = after + seg_recv[holders[j], k, pl.ds(places[j], 1), :]
+        weights.extend(reversed(ordered))
+    weight_cols = jnp.transpose(spread(jnp.concatenate(weights, axis=0), c * heads))
+    own.wait()
+    for copy in state_copies:
+        copy.wait_recv()
+    for j in range(per):
+        total = None
+        for k in range(n_ctx):
+            r = j * n_ctx + k
+            term = weight_cols[:, r : r + 1] * state_recv[holders[j], k].astype(F32)
+            total = term if total is None else total + term
+        start_state[j] = total
+
+    for copy in col_copies:
+        copy.wait_recv()
+    wide_pad = jnp.zeros((rows, all_cols - col_send.shape[1]), F32)
+    columns = jnp.zeros((rows, all_cols), F32)
+    for i in range(n_ctx * n_tp):
+        wide = jnp.concatenate([col_recv[i], wide_pad], axis=1)
+        columns = columns + (pltpu.roll(wide, n_cols * i, 1) if i else wide)
+    bcfull[lead : lead + rows, :] = columns[:, :width]
+    conv = cbb_ref[...]
+    for k in range(taps):
+        conv = conv + cbw_ref[k : k + 1, :] * bcfull[k * per : k * per + rows, :]
+    bcc = silu(conv)
+    b_all, c_all = bcc[:, :state_n], bcc[:, state_n:]
+    head_first = (p * n_ctx + c) * heads
+    step_size = softplus(spread(columns[:, width:], head_first) + dtb_row)
+    log_keep = step_size * rate_row
+    driven = step_size * xc
+
+    row_slot = lax.rem(lax.broadcasted_iota(jnp.int32, (rows, 1), 0), per)
+    from_start = jnp.zeros((rows, chans), F32)
+    c_low = c_all.astype(BF16)
+    for j in range(per):
+        from_start += jnp.where(row_slot == j, nt_dot(c_low, start_state[j].astype(BF16)), 0.0)
+
+    def at(value, t):
+        return value[t * per : (t + 1) * per]
+
+    total = jnp.zeros((per, chans), F32)
+    sums = []
+    for t in range(steps):
+        total = total + at(log_keep, t)
+        sums.append(total)
+    for t in range(steps):
+        y = jnp.exp(sums[t]) * at(from_start, t) + skip_row * at(xc, t)
+        for s in range(t + 1):
+            overlap = jnp.sum(at(b_all, s) * at(c_all, t), axis=1, keepdims=True)
+            term = at(driven, s) * overlap
+            y = y + (term if s == t else jnp.exp(sums[t] - sums[s]) * term)
+        gated_ref[t * per : (t + 1) * per, :] = y
+    gated = gated_ref[...] * z_gate
+    squares = jnp.sum(gated * gated, axis=1, keepdims=True)
+    sq_send[...] = jnp.broadcast_to(squares, sq_send.shape)
+    sq_copies = [send(sq_send, sq_recv.at[mine], sq_sems, i, o) for i, o in enumerate(group)]
+    sq_recv[mine] = sq_send[...]
+
+    loads[4].wait()
+    partial = jnp.dot((gated * gate_row).astype(BF16), wout[...], preferred_element_type=F32)
+    for i in range(n_ctx * n_tp):
+        out_send[i] = partial[:, i * feats : (i + 1) * feats].astype(BF16)
+    out_copies = []
+    for i, o in enumerate(group):
+        pc, _, pp = peer(o)
+        out_copies.append(send(out_send.at[pc * n_tp + pp], out_recv.at[mine], out_sems, i, o))
+    out_recv[mine] = out_send[mine]
+
+    late = [jnp.exp(sums[-1] - sums[t]) * at(driven, t) for t in range(steps)]
+    flat_rows = jnp.concatenate(late + [jnp.exp(sums[-1])] * (rows // per), axis=0)
+    tall = jnp.transpose(flat_rows)
+    for j in range(per):
+        b_own = jnp.where(row_slot == j, b_all, 0.0)
+        final_ref[j] = (
+            tall[:, rows + j : rows + j + 1] * start_state[j] + f32_dot(tall[:, :rows], b_own)
+        )
+
+    for copy in sq_copies + out_copies:
+        copy.wait_recv()
+    total_squares = sq_recv[0]
+    mixed = out_recv[0].astype(F32)
+    for i in range(1, n_ctx * n_tp):
+        total_squares = total_squares + sq_recv[i]
+        mixed = mixed + out_recv[i].astype(F32)
+    inverse = lax.rsqrt(total_squares[:, 0:1] / (total_heads * dim) + epsilon)
+    mixed = mixed * inverse
+    for t in range(steps):
+        mixed_ref[t] = at(mixed, t).astype(BF16)
+    for copy in (
+        emb_copies + seg_copies + xt_copies + bt_copies + state_copies + col_copies + sq_copies
+        + out_copies
+    ):
+        copy.wait_send()
+
+
+def kernel_device(
+    sizes,
+    token_ids,
+    decode_prompt,
+    embedding,
+    norm_gain,
+    w_zx,
+    w_bcdt,
+    conv_x_weight,
+    conv_x_bias,
+    conv_bc_weight,
+    conv_bc_bias,
+    dt_bias,
+    a_log,
+    d_skip,
+    gate_norm_gain,
+    w_out,
+    state_parts,
+    seg_rate,
+    x_tail,
+    bc_tail,
+):
+    n_ctx, n_dp, n_tp, _ = sizes
+    steps = token_ids.shape[0]
+    slots = decode_prompt.shape[0]
+    per = state_parts.shape[1]
+    rows = steps * per
+    vocab, feats = embedding.shape
+    heads, dim, model = w_zx.shape[1:]
+    chans = heads * dim
+    tp_heads, state_n = state_parts.shape[2], state_parts.shape[4]
+    world, ring = n_ctx * n_dp * n_tp, n_ctx * n_tp
+    smem = pl.BlockSpec(memory_space=pltpu.SMEM)
+    vmem = pl.BlockSpec(memory_space=pltpu.VMEM)
+    anywhere = pl.BlockSpec(memory_space=pl.ANY)
+    rest = max(1, vocab % ROW_TILE)
+    part = pl.pallas_call(
+        functools.partial(gather_kernel, steps, slots, n_dp),
+        out_shape=jax.ShapeDtypeStruct((n_dp, rows, feats), BF16),
+        in_specs=[smem, smem, anywhere],
+        out_specs=vmem,
+        scratch_shapes=[
+            pltpu.VMEM((steps * slots, ROW_TILE, feats), BF16),
+            pltpu.VMEM((rest, feats), BF16),
+            pltpu.SemaphoreType.DMA((steps * slots,)),
+            pltpu.SemaphoreType.DMA,
+        ],
+        name="gather_rows",
+    )(token_ids, decode_prompt, embedding)
+    sem = pltpu.SemaphoreType.DMA
+    wide = 2 * state_n
+    full_rows = -(-(conv_x_weight.shape[0] - 1 + steps) * per // 8) * 8
+    mixed, final = pl.pallas_call(
+        functools.partial(mixer_kernel, sizes),
+        out_shape=(
+            jax.ShapeDtypeStruct((steps, per, feats), BF16),
+            jax.ShapeDtypeStruct((per, chans, state_n), F32),
+        ),
+        in_specs=[smem] + [vmem] * 13 + [anywhere] * 4,
+        out_specs=(vmem, vmem),
+        scratch_shapes=[
+            pltpu.VMEM((2 * chans, model), BF16),
+            pltpu.VMEM(w_bcdt.shape, BF16),
+            pltpu.VMEM((chans, model), BF16),
+            pltpu.VMEM((per, tp_heads * dim, state_n), BF16),
+            pltpu.VMEM((n_dp, tp_heads * dim, state_n), BF16),
+            pltpu.VMEM((n_dp, n_ctx, chans, state_n), BF16),
+            pltpu.VMEM((n_dp, ring, rows, feats), BF16),
+            pltpu.VMEM((n_dp, n_ctx, per, tp_heads), F32),
+            pltpu.VMEM((n_dp,) + x_tail.shape, BF16),
+            pltpu.VMEM((n_dp,) + bc_tail.shape, BF16),
+            pltpu.VMEM((rows, 128), F32),
+            pltpu.VMEM((ring, rows, 128), F32),
+            pltpu.VMEM((rows, 128), F32),
+            pltpu.VMEM((ring, rows, 128), F32),
+            pltpu.VMEM((ring, rows, feats), BF16),
+            pltpu.VMEM((ring, rows, feats), BF16),
+            pltpu.VMEM((per, chans, state_n), F32),
+            pltpu.VMEM((full_rows, chans), F32),
+            pltpu.VMEM((full_rows, wide), F32),
+            pltpu.VMEM((rows, chans), F32),
+            sem((5,)),
+            sem,
+            sem((2, world)),
+            sem((2, n_ctx * n_dp)),
+            sem((2, n_ctx * n_dp)),
+            sem((2, n_dp)),
+            sem((2, n_dp)),
+            sem((2, ring)),
+            sem((2, ring)),
+            sem((2, ring)),
+        ],
+        compiler_params=pltpu.CompilerParams(
+            collective_id=0, has_side_effects=True, vmem_limit_bytes=56 * 1024 * 1024
+        ),
+        name="mixer",
+    )(
+        decode_prompt,
+        part,
+        norm_gain[None],
+        conv_x_weight,
+        conv_x_bias,
+        conv_bc_weight,
+        conv_bc_bias[None],
+        dt_bias[None],
+        a_log[None],
+        d_skip[None],
+        gate_norm_gain,
+        seg_rate,
+        x_tail,
+        bc_tail,
+        w_zx.reshape(2 * chans, model),
+        w_bcdt,
+        w_out.reshape(chans, model),
+        state_parts.reshape(per, tp_heads * dim, state_n),
+    )
+    return mixed, final.reshape(per, heads, dim, state_n)
+
+
+def choose_device(sizes, *args):
+    embedding, w_zx, w_bcdt = args[2], args[4], args[5]
+    heads, dim = w_zx.shape[1:3]
+    fits = (
+        embedding.shape[1] % 128 == 0
+        and (heads * dim) % 128 == 0
+        and w_bcdt.shape[1] <= 128
+        and embedding.shape[0] >= ROW_TILE
+    )
+    if fits:
+        return kernel_device(sizes, *args)
+    return per_device(*args)
+
+
 def solution(mesh):
+    sizes = (mesh.shape["ctx"], mesh.shape["dp"], mesh.shape["tp"], HEADS)
     return jax.shard_map(
-        per_device,
+        functools.partial(choose_device, sizes),
         mesh=mesh,
         in_specs=(
             P(),

time: 233 us -> 40.9 us (0.18)
  blocking collectives: 122 us -> 0 us
  waiting for transfers between devices: 50.4 us -> 0 us
  Pallas kernels: 0 us -> 34.1 us
  local copies, waits for them, and re-layouts: 20.9 us -> 5.8 us
  matrix products: 14.7 us -> 0 us
  between operations: 14.9 us -> 0.66 us
  other arithmetic: 5.73 us -> 0 us
  starting transfers between devices: 3.54 us -> 0 us
    all_gather x6 -> x0, blocking collectives: 85.5 us -> none  [the longest x1 32.8 us: per_device(): embedded = lax.all_gather(own_rows, ('ctx', 'tp'), axis=2, tiled=True)]
    unnamed x5 -> x0, waiting for transfers between devices: 44.5 us -> none
    pallas_call x0 -> x2, Pallas kernels: none -> 34.1 us  [the longest x1 31.5 us: kernel_device(): pl.pallas_call(functools.partial(mixer_kernel, sizes), out_shape=(jax.Sha...]
    psum x1 -> x0, blocking collectives: 31.9 us -> none  [per_device(): total_squares = lax.psum(local_squares, ('ctx', 'tp'))]
    dot_general x10 -> x0, matrix products: 14.7 us -> none  [the longest x1 6.79 us: per_device(): jnp.einsum('rd,khed->krhe', normed, w_zx, preferred_element_type=jnp.floa...]
    gather x2 -> x0, local copies, waits for them, and re-layouts: 6.9 us -> none  [per_device(): jnp.take(embedding, jnp.clip(offset_tokens, 0, vocab_rows - 1), axis=0)]
    all_to_all x1 -> x0, waiting for transfers between devices: 5.91 us -> none  [per_device(): lax.all_to_all(channel_sums.astype(jnp.bfloat16), 'ctx', split_axis=1, co...]
    unnamed x36 -> x6, local copies, waits for them, and re-layouts: 11.3 us -> 5.8 us
  transfers between devices with their start and end apart: 4 -> 0, of which waited for: 3 -> 0; matrix products, arithmetic and copies ran while one was open for 9% -> 0% of each run, Pallas kernels for 0% -> 0%
where the time goes in v1:
time: 40.9 us; the launch traced here: 40.5 us
  Pallas kernels  34.1 us (83%)
  local copies, waits for them, and re-layouts  5.8 us (14%)
  between operations  0.66 us (2%)
    pallas_call x1, Pallas kernels, kernel_device(): pl.pallas_call(functools.partial(mixer_kernel, sizes), out_shape=(jax.Sha...  31.5 us
    unnamed x6, local copies, waits for them, and re-layouts  5.8 us
    pallas_call x1, Pallas kernels, kernel_device(): pl.pallas_call(functools.partial(gather_kernel, steps, slots, n_dp), out_...  2.53 us

profile of v1, /device:TPU:0, one launch (start us, length us, event | category | flops | bytes accessed | tf_op | source)
XLA Modules:
  0.0 40.5 jit_solution(7859149168376701663)
XLA Ops:
  0.6 0.0 copy-start
  0.6 1.3 %copy.21.bt_ref = bf16[2,3,256]{2,1,0:T(4,128)(2,1)} copy(bf16[2,3,256]{2,0,1:T(2,128)(2,1)} %param.37) | data formatting | bytes 6144 | tf_op args[18]
  2.0 2.5 %gather_rows.1.part_ref = bf16[2,8,256]{2,1,0:T(8,128)(2,1)} custom-call(s32[4,4]{1,0:T(4,128)} %tok_ref.1, s32[4]{0:T(128)} %dec_ref.3, bf16[25140,256]{1,0:T(8,128)(2,1)} %emb_ref.1), custom_call_target="tpu_custom_call" | custom-call | tf_op jit(solution)/shard_map/gather_rows/pallas_call | solution.py:586
  4.5 0.0 copy-done
  4.5 1.3 %copy.22.wbc_hbm = bf16[4096,24]{1,0:T(8,128)(2,1)} copy(bf16[4096,24]{0,1:T(8,128)(2,1)S(1)} %copy-done) | data formatting | bytes 393216 | tf_op args[5]
  5.8 31.5 %mixer.1 = (bf16[4,2,256]{2,1,0:T(2,128)(2,1)}, f32[2,512,128]{2,1,0:T(8,128)}) custom-call(s32[4]{0:T(128)} %dec_ref.3, bf16[2,8,256]{2,1,0:T(8,128)(2,1)} %gather_rows.1.part_ref, f32[1,4096]{1,0:T(1,128)} %bitcast.13, f32[4,8,64]{2,1,0:T(8,128)} %cxw_ref.1, f32[8,64]{1,0:T(8,128)} %cxb_ref.1, f32[4,256]{1,0:T(4,128)} %cbw_ref.1, f32[1,256]{1,0:T(1,128)} %bitcast.14, ...), custom_call_target="tpu_custom_call" | custom-call | tf_op jit(solution)/shard_map/mixer/pallas_call | solution.py:602
  37.4 1.3 %copy.25 = bf16[4,2,256]{2,1,0:T(2,128)(2,1)} copy(bf16[4,2,256]{2,1,0:T(2,128)(2,1)} %get-tuple-element.8) | data formatting | bytes 8192
  38.6 1.9 %copy.26 = f32[2,8,64,128]{3,2,1,0:T(8,128)} copy(f32[2,8,64,128]{3,2,1,0:T(8,128)} %bitcast.12) | data formatting | bytes 1048576
Async XLA Ops:
  0.6 3.9 %copy-start = (bf16[4096,24]{0,1:T(8,128)(2,1)S(1)}, bf16[4096,24]{0,1:T(8,128)(2,1)}, u32[]{:S(2)}) copy-start(bf16[4096,24]{0,1:T(8,128)(2,1)} %param.24) | copy-start | bytes 589828

commit v2 on v1

--- a/solution.py
+++ b/solution.py
@@ -233,6 +233,24 @@
     sizes,
     dec_ref,
     part_ref,
+    seg_ref,
+    xt_ref,
+    bt_ref,
+    gain_hbm,
+    cxw_hbm,
+    cxb_hbm,
+    cbw_hbm,
+    cbb_hbm,
+    dtb_hbm,
+    alog_hbm,
+    skip_hbm,
+    gg_hbm,
+    wzx_hbm,
+    wbc_hbm,
+    wout_hbm,
+    state_hbm,
+    mixed_ref,
+    final_hbm,
     gain_ref,
     cxw_ref,
     cxb_ref,
@@ -242,15 +260,9 @@
     alog_ref,
     skip_ref,
     gg_ref,
-    seg_ref,
-    xt_ref,
-    bt_ref,
-    wzx_hbm,
-    wbc_hbm,
-    wout_hbm,
-    state_hbm,
-    mixed_ref,
     final_ref,
+    pair_recv,
+    pair_send,
     wzx,
     wbc,
     wout,
@@ -272,7 +284,10 @@
     bcfull,
     gated_ref,
     load_sems,
-    own_sem,
+    small_sems,
+    own_sems,
+    final_sem,
+    pair_sems,
     emb_sems,
     state_sems,
     seg_sems,
@@ -294,8 +309,30 @@
     taps = cxw_ref.shape[0]
     model = gain_ref.shape[1]
     tp_heads = seg_ref.shape[-1]
-    n_cols = wbc_hbm.shape[1]
+    n_cols = wbc_hbm.shape[0]
     all_cols = n_cols * n_ctx * n_tp
+
+    def peer(offset):
+        dc, dd, dt = offset
+        return lax.rem(c + dc, n_ctx), lax.rem(d + dd, n_dp), lax.rem(p + dt, n_tp)
+
+    def device(offset):
+        a, b, e = peer(offset)
+        return {"ctx": a, "dp": b, "tp": e}
+
+    everyone = [
+        (a, b, e) for a in range(n_ctx) for b in range(n_dp) for e in range(n_tp) if a + b + e
+    ]
+    everyone.sort(key=lambda o: -(min(o[2], n_tp - o[2]) * 4 + o[1] * 2 + o[0]))
+    group = [o for o in everyone if o[1] == 0]
+    beside = [o for o in group if o[2] == 0]
+    across = [o for o in everyone if o[0] == 0 and o[2] == 0]
+
+    barrier = pltpu.get_barrier_semaphore()
+    for o in everyone:
+        pl.semaphore_signal(
+            barrier, inc=1, device_id=device(o), device_id_type=pl.DeviceIdType.MESH
+        )
 
     loads = []
     half = wzx_hbm.shape[0] // 2
@@ -311,27 +348,32 @@
         load.start()
         loads.append(load)
 
-    def peer(offset):
-        dc, dd, dt = offset
-        return lax.rem(c + dc, n_ctx), lax.rem(d + dd, n_dp), lax.rem(p + dt, n_tp)
-
-    def device(offset):
-        a, b, e = peer(offset)
-        return {"ctx": a, "dp": b, "tp": e}
-
-    everyone = [
-        (a, b, e) for a in range(n_ctx) for b in range(n_dp) for e in range(n_tp) if a + b + e
-    ]
-    everyone.sort(key=lambda o: -(min(o[2], n_tp - o[2]) * 4 + o[1] * 2 + o[0]))
-    group = [o for o in everyone if o[1] == 0]
-    routed = [o for o in everyone if o[2] == 0]
-    across = [o for o in everyone if o[0] == 0 and o[2] == 0]
-
-    barrier = pltpu.get_barrier_semaphore()
-    for o in everyone:
-        pl.semaphore_signal(
-            barrier, inc=1, device_id=device(o), device_id_type=pl.DeviceIdType.MESH
-        )
+    small_pairs = (
+        (gain_hbm, gain_ref),
+        (cxw_hbm, cxw_ref),
+        (cxb_hbm, cxb_ref),
+        (cbw_hbm, cbw_ref),
+        (cbb_hbm, cbb_ref),
+        (dtb_hbm, dtb_ref),
+        (alog_hbm, alog_ref),
+        (skip_hbm, skip_ref),
+        (gg_hbm, gg_ref),
+    )
+    smalls = []
+    for i, (source, target) in enumerate(small_pairs):
+        load = pltpu.make_async_copy(source, target, small_sems.at[i])
+        load.start()
+        smalls.append(load)
+    owns = []
+    for source, target in (
+        (part_ref.at[d], emb_recv.at[d, mine]),
+        (seg_ref.at[0], seg_recv.at[c]),
+        (xt_ref, xt_recv.at[d]),
+        (bt_ref, bt_recv.at[d]),
+    ):
+        load = pltpu.make_async_copy(source, target, own_sems.at[len(owns)])
+        load.start()
+        owns.append(load)
 
     def send(source, target, sems, slot, offset):
         copy = pltpu.make_async_remote_copy(
@@ -346,12 +388,14 @@
         return copy
 
     loads[0].wait()
+    picks = []
     for g in range(n_dp):
         pick = jnp.int32(0)
         for j in range(per):
             local = dec_ref[g * per + j] - d * per
             pick += jnp.where((local >= 0) & (local < per), local, 0)
         state_send[g] = state_in[pick]
+        picks.append(pick)
 
     col_send[...] = jnp.zeros_like(col_send)
 
@@ -361,26 +405,30 @@
         send(part_ref.at[peer(o)[1]], emb_recv.at[d, mine], emb_sems, i, o)
         for i, o in enumerate(everyone)
     ]
-    emb_recv[d, mine] = part_ref[d]
-    seg_copies = [send(seg_ref.at[0], seg_recv.at[d, c], seg_sems, i, o) for i, o in enumerate(routed)]
+    seg_copies = [send(seg_ref.at[0], seg_recv.at[c], seg_sems, i, o) for i, o in enumerate(beside)]
+    parity = lax.rem(c, 2)
+    mate = c + 1 - 2 * parity
+
+    def owned(ref, g, owner):
+        return ref.at[g, pl.ds(pl.multiple_of(owner * chans, chans), chans)]
+
+    pair_copies = []
+    for g in range(n_dp):
+        for m in range(n_ctx // 2):
+            slot = g * (n_ctx // 2) + m
+            copy = pltpu.make_async_remote_copy(
+                src_ref=owned(state_send, g, 2 * m + 1 - parity),
+                dst_ref=pair_recv.at[g, m],
+                send_sem=pair_sems.at[0, slot],
+                recv_sem=pair_sems.at[1, slot],
+                device_id={"ctx": mate, "dp": d, "tp": p},
+                device_id_type=pl.DeviceIdType.MESH,
+            )
+            copy.start()
+            pair_copies.append(copy)
     xt_copies = [send(xt_ref, xt_recv.at[d], xt_sems, i, o) for i, o in enumerate(across)]
     bt_copies = [send(bt_ref, bt_recv.at[d], bt_sems, i, o) for i, o in enumerate(across)]
-    state_copies = []
-    for i, o in enumerate(routed):
-        pc, pd, _ = peer(o)
-        source = state_send.at[pd, pl.ds(pl.multiple_of(pc * chans, chans), chans)]
-        state_copies.append(send(source, state_recv.at[d, c], state_sems, i, o))
-    own = pltpu.make_async_copy(
-        state_send.at[d, pl.ds(pl.multiple_of(c * chans, chans), chans)],
-        state_recv.at[d, c],
-        own_sem,
-    )
-    own.start()
-    seg_recv[d, c] = seg_ref[0]
-    xt_recv[d] = xt_ref[...]
-    bt_recv[d] = bt_ref[...]
-
-    lane = lax.broadcasted_iota(jnp.int32, (1, chans), 1)
+
     fold = (
         lax.broadcasted_iota(jnp.int32, (dim, chans), 0)
         == lax.rem(lax.broadcasted_iota(jnp.int32, (dim, chans), 1), dim)
@@ -400,6 +448,43 @@
         ).astype(F32)
         return f32_dot(value, chosen)
 
+    owns[1].wait()
+    for copy in seg_copies:
+        copy.wait_recv()
+    decays = []
+    for device_at in (c, mate):
+        for g in range(n_dp):
+            after = jnp.zeros((1, tp_heads), F32)
+            for k in range(n_ctx):
+                after += jnp.where(k > device_at, seg_recv[k, pl.ds(picks[g], 1), :], 0.0)
+            decays.append(jnp.exp(-after))
+    decays = jnp.concatenate(decays, axis=0)
+    decay_cols = [
+        jnp.transpose(spread(decays, (2 * m + parity) * heads)) for m in range(n_ctx // 2)
+    ]
+    for g in range(n_dp):
+        for m in range(n_ctx // 2):
+            pair_copies[g * (n_ctx // 2) + m].wait_recv()
+            first = pl.multiple_of((2 * m + parity) * chans, chans)
+            here = state_send[g, pl.ds(first, chans), :].astype(F32)
+            pair_send[g, m] = (
+                decay_cols[m][:, g : g + 1] * here
+                + decay_cols[m][:, n_dp + g : n_dp + g + 1] * pair_recv[g, m].astype(F32)
+            ).astype(BF16)
+    state_copies = []
+    for a in range(n_ctx // 2):
+        for b in range(n_dp):
+            if a + b:
+                o = (2 * a, b, 0)
+                pc, pd, _ = peer(o)
+                source = pair_send.at[pd, lax.div(pc, 2)]
+                slot = b * (n_ctx // 2) + a
+                target = state_recv.at[d, lax.div(c, 2)]
+                state_copies.append(send(source, target, state_sems, slot, o))
+    state_recv[d, lax.div(c, 2)] = pair_send[d, lax.div(c, 2)]
+
+    for load in smalls:
+        load.wait()
     tap_rows = [flat(cxw_ref[k]) for k in range(taps)]
     bias_row = flat(cxb_ref[...])
     gate_row = flat(gg_ref[...])
@@ -407,6 +492,7 @@
     rate_row = -jnp.exp(spread(alog_ref[...], 0))
     skip_row = spread(skip_ref[...], 0)
 
+    owns[0].wait()
     for copy in emb_copies:
         copy.wait_recv()
     pieces = []
@@ -419,7 +505,7 @@
     scale = lax.rsqrt(jnp.sum(embedded * embedded, axis=1, keepdims=True) / model + epsilon)
     normed = (embedded * scale * gain_ref[...]).astype(BF16)
     loads[1].wait()
-    col_send[:, 0:n_cols] = jnp.dot(normed, wbc[...], preferred_element_type=F32)
+    col_send[:, 0:n_cols] = nt_dot(normed, wbc[...])
     col_copies = [send(col_send, col_recv.at[mine], col_sems, i, o) for i, o in enumerate(group)]
     col_recv[mine] = col_send[...]
     loads[2].wait()
@@ -427,15 +513,21 @@
     loads[3].wait()
     z_gate = silu(nt_dot(normed, wzx[0:half, :]))
 
+    owns[2].wait()
+    owns[3].wait()
     for copy in xt_copies + bt_copies:
         copy.wait_recv()
     holders = [lax.div(dec_ref[d * per + j], per) for j in range(per)]
     places = [lax.rem(dec_ref[d * per + j], per) for j in range(per)]
+    plane_rows = lax.broadcasted_iota(jnp.int32, (per, 1), 0)
     for k in range(taps - 1):
         for j in range(per):
             r = k * per + j
             xfull[r : r + 1, :] = flat(xt_recv[holders[j], places[j], k].astype(F32))
-            bcfull[r : r + 1, :] = bt_recv[holders[j], places[j], pl.ds(k, 1), :].astype(F32)
+            plane = bt_recv[holders[j], k].astype(F32)
+            bcfull[r : r + 1, :] = jnp.sum(
+                jnp.where(plane_rows == places[j], plane, 0.0), axis=0, keepdims=True
+            )
     lead = (taps - 1) * per
     xfull[lead : lead + rows, :] = x_rows
     conv = bias_row
@@ -443,27 +535,13 @@
         conv = conv + tap_rows[k] * xfull[k * per : k * per + rows, :]
     xc = silu(conv)
 
-    for copy in seg_copies:
-        copy.wait_recv()
-    weights = []
-    for j in range(per):
-        after = jnp.zeros((1, tp_heads), F32)
-        ordered = []
-        for k in reversed(range(n_ctx)):
-            ordered.append(jnp.exp(-after))
-            after = after + seg_recv[holders[j], k, pl.ds(places[j], 1), :]
-        weights.extend(reversed(ordered))
-    weight_cols = jnp.transpose(spread(jnp.concatenate(weights, axis=0), c * heads))
-    own.wait()
     for copy in state_copies:
         copy.wait_recv()
     for j in range(per):
-        total = None
-        for k in range(n_ctx):
-            r = j * n_ctx + k
-            term = weight_cols[:, r : r + 1] * state_recv[holders[j], k].astype(F32)
-            total = term if total is None else total + term
-        start_state[j] = total
+        begin = state_recv[holders[j], 0].astype(F32)
+        for m in range(1, n_ctx // 2):
+            begin += state_recv[holders[j], m].astype(F32)
+        start_state[j] = begin
 
     for copy in col_copies:
         copy.wait_recv()
@@ -529,6 +607,9 @@
             tall[:, rows + j : rows + j + 1] * start_state[j] + f32_dot(tall[:, :rows], b_own)
         )
 
+    final_copy = pltpu.make_async_copy(final_ref, final_hbm, final_sem)
+    final_copy.start()
+
     for copy in sq_copies + out_copies:
         copy.wait_recv()
     total_squares = sq_recv[0]
@@ -541,10 +622,31 @@
     for t in range(steps):
         mixed_ref[t] = at(mixed, t).astype(BF16)
     for copy in (
-        emb_copies + seg_copies + xt_copies + bt_copies + state_copies + col_copies + sq_copies
+        emb_copies + seg_copies + pair_copies + xt_copies + bt_copies + state_copies + col_copies + sq_copies
         + out_copies
     ):
         copy.wait_send()
+    final_copy.wait()
+
+
+def tail_kernel(mixed_in, final_in, mixed_out, final_out, mixed_buf, final_buf, in_sems, out_sems):
+    moves = [(mixed_in, mixed_buf, mixed_out)]
+    cuts = 4 if final_in.shape[1] % 32 == 0 else 1
+    size = final_in.shape[1] // cuts
+    for j in range(final_in.shape[0]):
+        for k in range(cuts):
+            piece = (j, pl.ds(k * size, size))
+            moves.append((final_in.at[piece], final_buf.at[piece], final_out.at[piece]))
+    moves = moves[1:] + moves[:1]
+    inward = [pltpu.make_async_copy(a, b, in_sems.at[i]) for i, (a, b, _) in enumerate(moves)]
+    outward = [pltpu.make_async_copy(b, e, out_sems.at[i]) for i, (_, b, e) in enumerate(moves)]
+    for copy in inward:
+        copy.start()
+    for first, second in zip(inward, outward):
+        first.wait()
+        second.start()
+    for copy in outward:
+        copy.wait()
 
 
 def kernel_device(
@@ -599,25 +701,43 @@
     sem = pltpu.SemaphoreType.DMA
     wide = 2 * state_n
     full_rows = -(-(conv_x_weight.shape[0] - 1 + steps) * per // 8) * 8
+    smalls = (
+        norm_gain[None],
+        conv_x_weight,
+        conv_x_bias,
+        conv_bc_weight,
+        conv_bc_bias[None],
+        dt_bias[None],
+        a_log[None],
+        d_skip[None],
+        gate_norm_gain,
+    )
+    bc_planes = jnp.swapaxes(bc_tail, 0, 1)
+    outs = (
+        jax.ShapeDtypeStruct((steps, per, feats), BF16),
+        jax.ShapeDtypeStruct((per, chans, state_n), F32),
+    )
+    pairs = n_ctx // 2
     mixed, final = pl.pallas_call(
         functools.partial(mixer_kernel, sizes),
-        out_shape=(
-            jax.ShapeDtypeStruct((steps, per, feats), BF16),
-            jax.ShapeDtypeStruct((per, chans, state_n), F32),
-        ),
-        in_specs=[smem] + [vmem] * 13 + [anywhere] * 4,
-        out_specs=(vmem, vmem),
+        out_shape=outs,
+        in_specs=[smem] + [anywhere] * 17,
+        out_specs=(vmem, anywhere),
         scratch_shapes=[
+            *[pltpu.VMEM(small.shape, small.dtype) for small in smalls],
+            pltpu.VMEM((per, chans, state_n), F32),
+            pltpu.VMEM((n_dp, pairs, chans, state_n), BF16),
+            pltpu.VMEM((n_dp, pairs, chans, state_n), BF16),
             pltpu.VMEM((2 * chans, model), BF16),
-            pltpu.VMEM(w_bcdt.shape, BF16),
+            pltpu.VMEM(w_bcdt.shape[::-1], BF16),
             pltpu.VMEM((chans, model), BF16),
             pltpu.VMEM((per, tp_heads * dim, state_n), BF16),
             pltpu.VMEM((n_dp, tp_heads * dim, state_n), BF16),
-            pltpu.VMEM((n_dp, n_ctx, chans, state_n), BF16),
+            pltpu.VMEM((n_dp, pairs, chans, state_n), BF16),
             pltpu.VMEM((n_dp, ring, rows, feats), BF16),
-            pltpu.VMEM((n_dp, n_ctx, per, tp_heads), F32),
+            pltpu.VMEM((n_ctx, per, tp_heads), F32),
             pltpu.VMEM((n_dp,) + x_tail.shape, BF16),
-            pltpu.VMEM((n_dp,) + bc_tail.shape, BF16),
+            pltpu.VMEM((n_dp,) + bc_planes.shape, BF16),
             pltpu.VMEM((rows, 128), F32),
             pltpu.VMEM((ring, rows, 128), F32),
             pltpu.VMEM((rows, 128), F32),
@@ -629,10 +749,13 @@
             pltpu.VMEM((full_rows, wide), F32),
             pltpu.VMEM((rows, chans), F32),
             sem((5,)),
+            sem((len(smalls),)),
+            sem((4,)),
             sem,
+            sem((2, n_dp * pairs)),
             sem((2, world)),
-            sem((2, n_ctx * n_dp)),
-            sem((2, n_ctx * n_dp)),
+            sem((2, n_dp * pairs)),
+            sem((2, n_ctx)),
             sem((2, n_dp)),
             sem((2, n_dp)),
             sem((2, ring)),
@@ -646,23 +769,28 @@
     )(
         decode_prompt,
         part,
-        norm_gain[None],
-        conv_x_weight,
-        conv_x_bias,
-        conv_bc_weight,
-        conv_bc_bias[None],
-        dt_bias[None],
-        a_log[None],
-        d_skip[None],
-        gate_norm_gain,
         seg_rate,
         x_tail,
-        bc_tail,
+        bc_planes,
+        *smalls,
         w_zx.reshape(2 * chans, model),
-        w_bcdt,
+        w_bcdt.T,
         w_out.reshape(chans, model),
         state_parts.reshape(per, tp_heads * dim, state_n),
     )
+    mixed, final = pl.pallas_call(
+        tail_kernel,
+        out_shape=outs,
+        in_specs=[anywhere] * 2,
+        out_specs=(anywhere, anywhere),
+        scratch_shapes=[
+            pltpu.VMEM(outs[0].shape, BF16),
+            pltpu.VMEM(outs[1].shape, F32),
+            sem((4 * per + 1,)),
+            sem((4 * per + 1,)),
+        ],
+        name="tail",
+    )(mixed, final)
     return mixed, final.reshape(per, heads, dim, state_n)
 
 
@@ -671,6 +799,7 @@
     heads, dim = w_zx.shape[1:3]
     fits = (
         embedding.shape[1] % 128 == 0
+        and sizes[0] % 2 == 0
         and (heads * dim) % 128 == 0
         and w_bcdt.shape[1] <= 128
         and embedding.shape[0] >= ROW_TILE

time: 40.9 us -> 33.7 us (0.82)
  local copies, waits for them, and re-layouts: 5.8 us -> 0 us
  Pallas kernels: 34.1 us -> 32.7 us
    unnamed x6 -> x0, local copies, waits for them, and re-layouts: 5.8 us -> none
    pallas_call x1 -> x2, Pallas kernels: 31.5 us -> 30 us  [the longest x1 28.2 us: kernel_device(): pl.pallas_call(functools.partial(mixer_kernel, sizes), out_shape=outs, in...]
where the time goes in v2:
time: 33.7 us; the launch traced here: 33.4 us
  Pallas kernels  32.7 us (97%)
  between operations  0.65 us (2%)
    pallas_call x1, Pallas kernels, kernel_device(): pl.pallas_call(functools.partial(mixer_kernel, sizes), out_shape=outs, in...  28.2 us
    pallas_call x1, Pallas kernels, kernel_device(): pl.pallas_call(functools.partial(gather_kernel, steps, slots, n_dp), out_...  2.68 us
    pallas_call x1, Pallas kernels, kernel_device(): pl.pallas_call(tail_kernel, out_shape=outs, in_specs=[anywhere] * 2, out_...  1.85 us

profile of v2, /device:TPU:0, one launch (start us, length us, event | category | flops | bytes accessed | tf_op | source)
XLA Modules:
  0.0 33.4 jit_solution(5625577027731867085)
XLA Ops:
  0.6 2.7 %gather_rows.1.part_ref = bf16[2,8,256]{2,1,0:T(8,128)(2,1)} custom-call(s32[4,4]{1,0:T(4,128)} %tok_ref.1, s32[4]{0:T(128)} %dec_ref.3, bf16[25140,256]{1,0:T(8,128)(2,1)} %emb_ref.1), custom_call_target="tpu_custom_call" | custom-call | tf_op jit(solution)/shard_map/gather_rows/pallas_call | solution.py:688
  3.3 28.2 %mixer.1 = (bf16[4,2,256]{2,1,0:T(2,128)(2,1)}, f32[2,512,128]{2,1,0:T(8,128)}) custom-call(s32[4]{0:T(128)} %dec_ref.3, bf16[2,8,256]{2,1,0:T(8,128)(2,1)} %gather_rows.1.part_ref, f32[1,2,32]{2,1,0:T(2,128)} %seg_ref.1, bf16[2,3,8,64]{3,2,1,0:T(8,128)(2,1)} %xt_ref.1, bf16[3,2,256]{2,1,0:T(2,128)(2,1)} %bitcast.16, f32[1,4096]{1,0:T(1,128)} %bitcast.15, ...), custom_call_target="tpu_custom_call" | custom-call | tf_op jit(solution)/shard_map/mixer/pallas_call | solution.py:721
  31.5 1.9 %tail.1 = (bf16[4,2,256]{2,1,0:T(2,128)(2,1)}, f32[2,512,128]{2,1,0:T(8,128)}) custom-call(bf16[4,2,256]{2,1,0:T(2,128)(2,1)} %get-tuple-element.6.mixed_in, f32[2,512,128]{2,1,0:T(8,128)} %get-tuple-element.7.final_in), custom_call_target="tpu_custom_call" | custom-call | tf_op jit(solution)/shard_map/tail/pallas_call | solution.py:781

commit v3 on v2

--- a/solution.py
+++ b/solution.py
@@ -288,6 +288,8 @@
     own_sems,
     final_sem,
     pair_sems,
+    seg_mate,
+    seg_own,
     emb_sems,
     state_sems,
     seg_sems,
@@ -325,7 +327,7 @@
     ]
     everyone.sort(key=lambda o: -(min(o[2], n_tp - o[2]) * 4 + o[1] * 2 + o[0]))
     group = [o for o in everyone if o[1] == 0]
-    beside = [o for o in group if o[2] == 0]
+    routed = [o for o in everyone if o[2] == 0]
     across = [o for o in everyone if o[0] == 0 and o[2] == 0]
 
     barrier = pltpu.get_barrier_semaphore()
@@ -367,9 +369,10 @@
     owns = []
     for source, target in (
         (part_ref.at[d], emb_recv.at[d, mine]),
-        (seg_ref.at[0], seg_recv.at[c]),
+        (seg_ref.at[0], seg_recv.at[d, c]),
         (xt_ref, xt_recv.at[d]),
         (bt_ref, bt_recv.at[d]),
+        (seg_ref.at[0], seg_own),
     ):
         load = pltpu.make_async_copy(source, target, own_sems.at[len(owns)])
         load.start()
@@ -389,12 +392,13 @@
 
     loads[0].wait()
     picks = []
-    for g in range(n_dp):
+    for b in range(n_dp):
+        target_group = lax.rem(d + b, n_dp)
         pick = jnp.int32(0)
         for j in range(per):
-            local = dec_ref[g * per + j] - d * per
+            local = dec_ref[target_group * per + j] - d * per
             pick += jnp.where((local >= 0) & (local < per), local, 0)
-        state_send[g] = state_in[pick]
+        state_send[b] = state_in[pick]
         picks.append(pick)
 
     col_send[...] = jnp.zeros_like(col_send)
@@ -405,27 +409,30 @@
         send(part_ref.at[peer(o)[1]], emb_recv.at[d, mine], emb_sems, i, o)
         for i, o in enumerate(everyone)
     ]
-    seg_copies = [send(seg_ref.at[0], seg_recv.at[c], seg_sems, i, o) for i, o in enumerate(beside)]
     parity = lax.rem(c, 2)
     mate = c + 1 - 2 * parity
-
-    def owned(ref, g, owner):
-        return ref.at[g, pl.ds(pl.multiple_of(owner * chans, chans), chans)]
-
+    blocks = [(a, b) for a in reversed(range(n_ctx // 2)) for b in reversed(range(n_dp))]
+
+    def to_mate(source, target, slot):
+        copy = pltpu.make_async_remote_copy(
+            src_ref=source,
+            dst_ref=target,
+            send_sem=pair_sems.at[0, slot],
+            recv_sem=pair_sems.at[1, slot],
+            device_id={"ctx": mate, "dp": d, "tp": p},
+            device_id_type=pl.DeviceIdType.MESH,
+        )
+        copy.start()
+        return copy
+
+    mate_copy = to_mate(seg_ref.at[0], seg_mate, len(blocks))
     pair_copies = []
-    for g in range(n_dp):
-        for m in range(n_ctx // 2):
-            slot = g * (n_ctx // 2) + m
-            copy = pltpu.make_async_remote_copy(
-                src_ref=owned(state_send, g, 2 * m + 1 - parity),
-                dst_ref=pair_recv.at[g, m],
-                send_sem=pair_sems.at[0, slot],
-                recv_sem=pair_sems.at[1, slot],
-                device_id={"ctx": mate, "dp": d, "tp": p},
-                device_id_type=pl.DeviceIdType.MESH,
-            )
-            copy.start()
-            pair_copies.append(copy)
+    for slot, (a, b) in enumerate(blocks):
+        first = pl.multiple_of(lax.rem(mate + 2 * a, n_ctx) * chans, chans)
+        source = state_send.at[b, pl.ds(first, chans)]
+        pair_copies.append(to_mate(source, pair_recv.at[b, a], slot))
+    pair_copies.append(mate_copy)
+    seg_copies = [send(seg_ref.at[0], seg_recv.at[d, c], seg_sems, i, o) for i, o in enumerate(routed)]
     xt_copies = [send(xt_ref, xt_recv.at[d], xt_sems, i, o) for i, o in enumerate(across)]
     bt_copies = [send(bt_ref, bt_recv.at[d], bt_sems, i, o) for i, o in enumerate(across)]
 
@@ -448,40 +455,33 @@
         ).astype(F32)
         return f32_dot(value, chosen)
 
-    owns[1].wait()
-    for copy in seg_copies:
-        copy.wait_recv()
-    decays = []
-    for device_at in (c, mate):
-        for g in range(n_dp):
-            after = jnp.zeros((1, tp_heads), F32)
-            for k in range(n_ctx):
-                after += jnp.where(k > device_at, seg_recv[k, pl.ds(picks[g], 1), :], 0.0)
-            decays.append(jnp.exp(-after))
-    decays = jnp.concatenate(decays, axis=0)
-    decay_cols = [
-        jnp.transpose(spread(decays, (2 * m + parity) * heads)) for m in range(n_ctx // 2)
+    owns[4].wait()
+    mate_copy.wait_recv()
+    shrink = []
+    for b in range(n_dp):
+        row = pl.ds(picks[b], 1)
+        shrink.append(jnp.exp(-jnp.where(parity == 0, seg_mate[row, :], seg_own[row, :])))
+    ones = [jnp.ones((1, tp_heads), F32)] * n_dp
+    shrink = jnp.concatenate(shrink + ones, axis=0)
+    shrink_cols = [
+        jnp.transpose(spread(shrink, lax.rem(c + 2 * a, n_ctx) * heads)) for a in range(n_ctx // 2)
     ]
-    for g in range(n_dp):
-        for m in range(n_ctx // 2):
-            pair_copies[g * (n_ctx // 2) + m].wait_recv()
-            first = pl.multiple_of((2 * m + parity) * chans, chans)
-            here = state_send[g, pl.ds(first, chans), :].astype(F32)
-            pair_send[g, m] = (
-                decay_cols[m][:, g : g + 1] * here
-                + decay_cols[m][:, n_dp + g : n_dp + g + 1] * pair_recv[g, m].astype(F32)
-            ).astype(BF16)
     state_copies = []
-    for a in range(n_ctx // 2):
-        for b in range(n_dp):
-            if a + b:
-                o = (2 * a, b, 0)
-                pc, pd, _ = peer(o)
-                source = pair_send.at[pd, lax.div(pc, 2)]
-                slot = b * (n_ctx // 2) + a
-                target = state_recv.at[d, lax.div(c, 2)]
-                state_copies.append(send(source, target, state_sems, slot, o))
-    state_recv[d, lax.div(c, 2)] = pair_send[d, lax.div(c, 2)]
+    for slot, (a, b) in enumerate(blocks):
+        pair_copies[slot].wait_recv()
+        first = pl.multiple_of(lax.rem(c + 2 * a, n_ctx) * chans, chans)
+        here = state_send[b, pl.ds(first, chans), :].astype(F32)
+        there = pair_recv[b, a].astype(F32)
+        factor = shrink_cols[a][:, b : b + 1]
+        even = jnp.where(parity == 0, here, there)
+        odd = jnp.where(parity == 0, there, here)
+        added = (factor * even + odd).astype(BF16)
+        target = state_recv.at[d, lax.div(c, 2)]
+        if a + b:
+            pair_send[b, a] = added
+            state_copies.append(send(pair_send.at[b, a], target, state_sems, slot, (2 * a, b, 0)))
+        else:
+            state_recv[d, lax.div(c, 2)] = added
 
     for load in smalls:
         load.wait()
@@ -535,12 +535,28 @@
         conv = conv + tap_rows[k] * xfull[k * per : k * per + rows, :]
     xc = silu(conv)
 
+    owns[1].wait()
+    for copy in seg_copies:
+        copy.wait_recv()
+    weights = []
+    for j in range(per):
+        after = jnp.zeros((1, tp_heads), F32)
+        ordered = []
+        row = pl.ds(places[j], 1)
+        for m in reversed(range(n_ctx // 2)):
+            ordered.append(jnp.exp(-after))
+            for k in (2 * m + 1, 2 * m):
+                after = after + seg_recv[holders[j], k, row, :]
+        weights.extend(reversed(ordered))
+    weight_cols = jnp.transpose(spread(jnp.concatenate(weights, axis=0), c * heads))
     for copy in state_copies:
         copy.wait_recv()
     for j in range(per):
-        begin = state_recv[holders[j], 0].astype(F32)
-        for m in range(1, n_ctx // 2):
-            begin += state_recv[holders[j], m].astype(F32)
+        begin = None
+        for m in range(n_ctx // 2):
+            r = j * (n_ctx // 2) + m
+            term = weight_cols[:, r : r + 1] * state_recv[holders[j], m].astype(F32)
+            begin = term if begin is None else begin + term
         start_state[j] = begin
 
     for copy in col_copies:
@@ -735,7 +751,7 @@
             pltpu.VMEM((n_dp, tp_heads * dim, state_n), BF16),
             pltpu.VMEM((n_dp, pairs, chans, state_n), BF16),
             pltpu.VMEM((n_dp, ring, rows, feats), BF16),
-            pltpu.VMEM((n_ctx, per, tp_heads), F32),
+            pltpu.VMEM((n_dp, n_ctx, per, tp_heads), F32),
             pltpu.VMEM((n_dp,) + x_tail.shape, BF16),
             pltpu.VMEM((n_dp,) + bc_planes.shape, BF16),
             pltpu.VMEM((rows, 128), F32),
@@ -750,12 +766,14 @@
             pltpu.VMEM((rows, chans), F32),
             sem((5,)),
             sem((len(smalls),)),
-            sem((4,)),
+            sem((5,)),
             sem,
-            sem((2, n_dp * pairs)),
+            sem((2, n_dp * pairs + 1)),
+            pltpu.VMEM((per, tp_heads), F32),
+            pltpu.VMEM((per, tp_heads), F32),
             sem((2, world)),
             sem((2, n_dp * pairs)),
-            sem((2, n_ctx)),
+            sem((2, n_ctx * n_dp)),
             sem((2, n_dp)),
             sem((2, n_dp)),
             sem((2, ring)),

time: 33.7 us -> 32.4 us (0.961)
  Pallas kernels: 32.7 us -> 31.5 us
    pallas_call x1, Pallas kernels: 28.2 us -> 27.1 us  [kernel_device(): pl.pallas_call(functools.partial(mixer_kernel, sizes), out_shape=outs, in...]
where the time goes in v3:
time: 32.4 us; the launch traced here: 32.2 us
  Pallas kernels  31.5 us (97%)
  between operations  0.65 us (2%)
    pallas_call x1, Pallas kernels, kernel_device(): pl.pallas_call(functools.partial(mixer_kernel, sizes), out_shape=outs, in...  27.1 us
    pallas_call x1, Pallas kernels, kernel_device(): pl.pallas_call(functools.partial(gather_kernel, steps, slots, n_dp), out_...  2.55 us
    pallas_call x1, Pallas kernels, kernel_device(): pl.pallas_call(tail_kernel, out_shape=outs, in_specs=[anywhere] * 2, out_...  1.85 us

profile of v3, /device:TPU:0, one launch (start us, length us, event | category | flops | bytes accessed | tf_op | source)
XLA Modules:
  0.0 32.2 jit_solution(1662370961259430982)
XLA Ops:
  0.6 2.6 %gather_rows.1.part_ref = bf16[2,8,256]{2,1,0:T(8,128)(2,1)} custom-call(s32[4,4]{1,0:T(4,128)} %tok_ref.1, s32[4]{0:T(128)} %dec_ref.3, bf16[25140,256]{1,0:T(8,128)(2,1)} %emb_ref.1), custom_call_target="tpu_custom_call" | custom-call | tf_op jit(solution)/shard_map/gather_rows/pallas_call | solution.py:704
  3.2 27.1 %mixer.1 = (bf16[4,2,256]{2,1,0:T(2,128)(2,1)}, f32[2,512,128]{2,1,0:T(8,128)}) custom-call(s32[4]{0:T(128)} %dec_ref.3, bf16[2,8,256]{2,1,0:T(8,128)(2,1)} %gather_rows.1.part_ref, f32[1,2,32]{2,1,0:T(2,128)} %seg_ref.1, bf16[2,3,8,64]{3,2,1,0:T(8,128)(2,1)} %xt_ref.1, bf16[3,2,256]{2,1,0:T(2,128)(2,1)} %bitcast.16, f32[1,4096]{1,0:T(1,128)} %bitcast.15, ...), custom_call_target="tpu_custom_call" | custom-call | tf_op jit(solution)/shard_map/mixer/pallas_call | solution.py:737
  30.3 1.9 %tail.1 = (bf16[4,2,256]{2,1,0:T(2,128)(2,1)}, f32[2,512,128]{2,1,0:T(8,128)}) custom-call(bf16[4,2,256]{2,1,0:T(2,128)(2,1)} %get-tuple-element.6.mixed_in, f32[2,512,128]{2,1,0:T(8,128)} %get-tuple-element.7.final_in), custom_call_target="tpu_custom_call" | custom-call | tf_op jit(solution)/shard_map/tail/pallas_call | solution.py:799
